TPU v7x, 512 devices: a whole 4x4x16 slice. The times are simulated.
512 devices in a mesh: dp: 64 (over z, y_hi, core), tensor: 8 (over x, y_lo).
Axes of the slice: x: 4, y: 4 (y_hi: 2, y_lo: 2; y = y_hi * 2 + y_lo), z: 16, core: 2. Of those that a mesh axis runs over, the one named last changes fastest.
Arguments:
- context: bfloat16 [8192, 4096], P('dp', 'tensor'), may hold values from -6 to 6
- out_weight: bfloat16 [4096, 2048], P('tensor'), may hold values from -0.09375 to 0.09375
- residual_in: float32 [8192, 2048], P('dp', 'tensor')
- norm_gain: float32 [2048], P('tensor'), may hold values from 0.1 to 1.9
- expert_ids: int32 [8192, 8], P('dp'), may hold values from 0 to 63, all different within a row; in each aligned block of 128 rows (0 to 127, 128 to 255, ...) at most 24 rows name the same one
- expert_gates: float32 [8192, 8], P('dp'), may hold values from 0.05 to 1
- w_gate: bfloat16 [64, 1536, 2048], P('dp', 'tensor'), may hold values from -0.125 to 0.125
- w_up: bfloat16 [64, 1536, 2048], P('dp', 'tensor'), may hold values from -0.125 to 0.125
- w_down: bfloat16 [64, 1536, 2048], P('dp', None, 'tensor'), may hold values from -0.15625 to 0.15625
Outputs:
- attended: float32 [8192, 2048], P('dp', 'tensor')
- expert_mix: bfloat16 [8192, 2048], P('dp', 'tensor')
Inputs may be any that keep to these rules, and one draw needn't show every extreme that they name: `expert_ids`: each token names 8 different experts. The 128 tokens of one index of dp (aligned blocks of rows) name any one expert at most 24 times, a bound that some block reaches.
All inputs are finite; a program needn't handle non-finite values.
Results may differ from a plain program's by a relative error of at most 0.0071.
Values may be sent and summed in bfloat16 or wider, within the bound.
A program may use at most 64 MiB of HBM per device.

v0:
```python
import jax
import jax.numpy as jnp
from jax import lax
from jax.sharding import PartitionSpec as P

epsilon = 1e-06


def local(
    context, out_weight, residual_in, norm_gain, expert_ids, expert_gates, w_gate, w_up, w_down
):
    num_tokens, width_local = residual_in.shape
    summed_proj = lax.psum_scatter(
        jnp.einsum("th,hd->dt", context, out_weight, preferred_element_type=jnp.float32),
        "tensor",
        scatter_dimension=0,
        tiled=True,
    )
    attended = residual_in + summed_proj.T
    squares = lax.psum(jnp.sum(attended * attended, axis=1), "tensor")
    full_width = width_local * lax.axis_size("tensor")
    scaling = lax.rsqrt(squares / full_width + epsilon)
    normed = (attended * scaling[:, None] * norm_gain).astype(jnp.bfloat16)
    top_count = expert_ids.shape[1]
    num_experts = w_gate.shape[0] * lax.axis_size("dp")
    capacity = max(2, 3 * num_tokens * top_count // (2 * num_experts))
    flat_ids = expert_ids.reshape(-1)
    one_hot = (flat_ids[:, None] == jnp.arange(num_experts, dtype=jnp.int32)[None, :]).astype(
        jnp.int32
    )
    earlier = jnp.cumsum(one_hot, axis=0) - one_hot
    position = jnp.sum(earlier * one_hot, axis=1)
    slot_index = flat_ids * capacity + position
    pair_token = jnp.arange(num_tokens * top_count, dtype=jnp.int32) // top_count
    source_token = (
        jnp.full((num_experts * capacity,), num_tokens, jnp.int32).at[slot_index].set(pair_token)
    )
    gate_local = w_gate[0]
    up_local = w_up[0]
    down_local = w_down[0]
    full_rows = lax.all_gather(normed, "tensor", axis=1, tiled=True)
    padded_rows = jnp.concatenate(
        [full_rows, jnp.zeros((1, full_rows.shape[1]), jnp.bfloat16)], axis=0
    )
    outgoing = padded_rows[source_token].reshape(num_experts, capacity, full_rows.shape[1])
    received = lax.all_to_all(outgoing, "dp", split_axis=0, concat_axis=0, tiled=True)
    gate_val = jnp.einsum("scd,hd->sch", received, gate_local, preferred_element_type=jnp.float32)
    up_val = jnp.einsum("scd,hd->sch", received, up_local, preferred_element_type=jnp.float32)
    activation = (jax.nn.silu(gate_val) * up_val).astype(jnp.bfloat16)
    summed_out = jnp.einsum(
        "sch,hd->scd",
        lax.all_gather(activation, "tensor", axis=2, tiled=True),
        down_local,
        preferred_element_type=jnp.float32,
    )
    result = summed_out.astype(jnp.bfloat16)
    returned = lax.all_to_all(result, "dp", split_axis=0, concat_axis=0, tiled=True)
    flat_back = returned.reshape(num_experts * capacity, width_local)
    picked = flat_back[slot_index].reshape(num_tokens, top_count, width_local).astype(jnp.float32)
    weights = expert_gates / jnp.sum(expert_gates, axis=1, keepdims=True)
    expert_mix = jnp.sum(weights[:, :, None] * picked, axis=1).astype(jnp.bfloat16)
    return (attended, expert_mix)


def solution(mesh):
    return jax.shard_map(
        local,
        mesh=mesh,
        in_specs=(
            P("dp", "tensor"),
            P("tensor", None),
            P("dp", "tensor"),
            P("tensor"),
            P("dp", None),
            P("dp", None),
            P("dp", "tensor", None),
            P("dp", "tensor", None),
            P("dp", None, "tensor"),
        ),
        out_specs=(P("dp", "tensor"), P("dp", "tensor")),
        check_vma=False,
    )
```

profile of v0, /device:TPU:4, one launch (start us, length us, event | category | flops | bytes accessed | tf_op | source)
XLA Modules:
  0.0 700.0 jit_solution(4294117381571597590)
XLA Ops:
  7.2 0.0 copy-start
  7.2 0.0 copy-start.3
  7.2 0.0 reduce-scatter.2.cloned.1.call-start
  7.2 1.5 copy-done
  8.8 2.6 fusion.14
  11.4 0.0 copy-start.2
  11.4 0.0 copy-start.5
  11.4 0.0 reduce-scatter.2.cloned.1.call-update
  11.4 0.0 all-gather.2.cloned.1.call-start
  11.5 0.0 copy-done.3
  11.5 0.1 copy.27
  11.6 0.1 eq.29
  11.7 0.1 eq.25
  11.8 18.0 %reduce-window.6 = s32[64,8,128]{2,1,0:T(8,128)S(1)} reduce-window(s32[64,8,128]{2,1,0:T(8,128)S(1)} %fusion.8, s32[]{:T(128)} %constant.37.clone.1), window={size=1x1x128 pad=0_0x0_0x127_0}, to_apply=%region_4.5 | reduce-window | flops 8323072 | bytes 524292 | tf_op jit(solution)/shard_map/reduce-window
  29.8 0.1 slice.12
  29.9 0.1 copy.29
  30.1 0.1 copy.30
  30.2 0.1 copy.26
  30.3 0.1 mul.61
  30.4 0.0 copy-done.2
  30.4 0.1 copy.24
  30.5 0.1 broadcast_add_fusion
  30.7 0.1 fusion.7
  30.8 4.3 scatter_custom_fusion
  35.1 25.5 %reduce-scatter.2.cloned.1.call-done = f32[256,128]{1,0:T(8,128)} async-done(((f32[2048,128]{1,0:T(8,128)}), f32[256,128]{1,0:T(8,128)}) %reduce-scatter.2.cloned.1.call-update) | async-done | bytes 131088 | tf_op jit(solution)/shard_map/reduce_scatter | solution.py:13
  60.7 1.0 multiply_reduce_fusion
  61.6 16.2 %psum.7 = f32[128]{0:T(128)S(1)} all-reduce(f32[128]{0:T(128)S(1)} %get-tuple-element.8), channel_id=1, replica_groups=mesh['dp'=64,'tensor'=8] {'tensor'}, use_global_device_ids=true, to_apply=%region_3.0 | all-reduce | flops 128 | bytes 1024 | tf_op jit(solution)/shard_map/psum | solution.py:20
  77.8 0.0 copy-done.5
  77.9 0.1 multiply_convert_fusion.1
  78.0 29.5 %all_gather.6 = bf16[128,2048]{0,1:T(8,128)(2,1)S(1)} all-gather(bf16[128,256]{0,1:T(8,128)(2,1)S(1)} %multiply_convert_fusion.1), channel_id=1, replica_groups=mesh['dp'=64,'tensor'=8] {'tensor'}, dimensions={1}, use_global_device_ids=true | all-gather | bytes 589824 | tf_op jit(solution)/shard_map/all_gather | solution.py:41
  107.5 0.2 copy.35
  107.8 7.1 %gather_fusion = bf16[1536,2048]{1,0:T(8,128)(2,1)} fusion(bf16[129,2048]{1,0:T(8,128)(2,1)S(1)} %concatenate.3.clone, s32[2048]{0:T(1024)S(1)} %pad_clamp_fusion), kind=kCustom, calls=%fused_computation | custom fusion | bytes 12589056 | tf_op jit(solution)/shard_map/gather | solution.py:45
  114.9 0.0 copy-start.6
  114.9 296.8 %all_to_all.10 = bf16[64,24,2048]{2,1,0:T(8,128)(2,1)S(1)} all-to-all(bf16[64,24,2048]{2,1,0:T(8,128)(2,1)} %bitcast.46), channel_id=1, replica_groups=mesh['dp'=64,'tensor'=8] {'dp'}, dimensions={0} | all-to-all | bytes 12582912 | tf_op jit(solution)/shard_map/all_to_all | solution.py:46
  411.7 0.0 copy-done.6
  411.7 0.0 copy-start.7
  411.7 2.1 fusion.3
  413.8 0.0 copy-done.7
  413.8 2.3 multiply_convert_fusion
  416.1 1.8 copy.32
  417.9 0.0 all-gather.2.cloned.1.call-update
  417.9 0.0 copy-start.8
  417.9 188.0 %all-gather.2.cloned.1.call-done = bf16[64,24,1536]{0,1,2:T(8,128)(2,1)} async-done(((bf16[64,24,192]{0,1,2:T(8,128)(2,1)}), bf16[64,24,1536]{0,1,2:T(8,128)(2,1)}) %all-gather.2.cloned.1.call-update) | async-done | bytes 4718608 | tf_op jit(solution)/shard_map/all_gather | solution.py:52
  605.9 13.3 %copy.33 = bf16[64,24,1536]{2,1,0:T(8,128)(2,1)} copy(bf16[64,24,1536]{0,1,2:T(8,128)(2,1)} %all-gather.2.cloned.1.call-done) | data formatting | bytes 9437184 | tf_op jit(solution)/shard_map/all_gather | solution.py:52
  619.2 0.0 copy-done.8
  619.2 0.0 copy-start.4
  619.2 4.6 convolution_convert_fusion
  623.8 19.4 %all-to-all-start.1 = ((bf16[64,24,256]{2,1,0:T(8,128)(2,1)}), bf16[64,24,256]{2,1,0:T(8,128)(2,1)S(1)}, u32[]{:S(2)}, u32[]{:S(2)}) async-start(bf16[64,24,256]{2,1,0:T(8,128)(2,1)} %convolution_convert_fusion), calls=%async_computation.2 | async-start | bytes 1572864 | tf_op jit(solution)/shard_map/all_to_all | solution.py:57
  643.3 0.0 copy-done.4
  643.3 0.7 copy.25
  644.0 0.8 copy.34
  644.8 43.3 %all-to-all-done.1 = bf16[64,24,256]{2,1,0:T(8,128)(2,1)S(1)} async-done(((bf16[64,24,256]{2,1,0:T(8,128)(2,1)}), bf16[64,24,256]{2,1,0:T(8,128)(2,1)S(1)}, u32[]{:S(2)}, u32[]{:S(2)}) %all-to-all-start.1) | async-done | bytes 786464 | tf_op jit(solution)/shard_map/all_to_all | solution.py:57
  688.1 0.0 copy-start.1
  688.1 3.9 gather_fusion.1
  692.1 0.0 copy-done.1
  692.1 1.0 fusion
  (13 shorter events, 0.2 us)
Async XLA Ops:
  7.2 1.6 copy-start
  7.2 4.3 copy-start.3
  7.2 53.5 %reduce-scatter.2.cloned.1.call-start = ((), (), s32[]{:S(2)}) async-start(), calls=%async_computation.3 | async-start | bytes 1179648 | tf_op jit(solution)/shard_map/reduce_scatter | solution.py:13
  11.4 19.0 %copy-start.2 = (f32[128,256]{1,0:T(8,128)S(1)}, f32[128,256]{1,0:T(8,128)}, u32[]{:S(2)}) copy-start(f32[128,256]{1,0:T(8,128)} %param.11) | copy-start | bytes 393220
  11.4 66.5 %copy-start.5 = (f32[256]{0:T(256)S(1)}, f32[256]{0:T(256)}, u32[]{:S(2)}) copy-start(f32[256]{0:T(256)} %param.12) | copy-start | bytes 3076
  11.4 594.4 %all-gather.2.cloned.1.call-start = ((), (), s32[]{:S(2)}) async-start(), calls=%async_computation.4 | async-start | bytes 10616832 | tf_op jit(solution)/shard_map/all_gather | solution.py:52
  114.9 296.8 %copy-start.6 = (bf16[1,192,2048]{2,1,0:T(8,128)(2,1)S(1)}, bf16[1,192,2048]{2,1,0:T(8,128)(2,1)}, u32[]{:S(2)}) copy-start(bf16[1,192,2048]{2,1,0:T(8,128)(2,1)} %param.15) | copy-start | bytes 2359300
  411.7 2.1 copy-start.7
  417.9 201.3 %copy-start.8 = (bf16[1,1536,256]{2,1,0:T(8,128)(2,1)S(1)}, bf16[1,1536,256]{2,1,0:T(8,128)(2,1)}, u32[]{:S(2)}) copy-start(bf16[1,1536,256]{2,1,0:T(8,128)(2,1)} %param.17) | copy-start | bytes 2359300
  619.2 24.1 %copy-start.4 = (f32[128,8]{0,1:T(8,128)S(1)}, f32[128,8]{0,1:T(8,128)}, u32[]{:S(2)}) copy-start(f32[128,8]{0,1:T(8,128)} %param.14) | copy-start | bytes 12292
  623.8 64.3 %all-to-all-start.1 = ((bf16[64,24,256]{2,1,0:T(8,128)(2,1)}), bf16[64,24,256]{2,1,0:T(8,128)(2,1)S(1)}, u32[]{:S(2)}, u32[]{:S(2)}) async-start(bf16[64,24,256]{2,1,0:T(8,128)(2,1)} %convolution_convert_fusion), calls=%async_computation.2 | async-start | bytes 1572864 | tf_op jit(solution)/shard_map/all_to_all | solution.py:57
  688.1 3.9 copy-start.1
Sparse Core Ops, SparseCore 0:
  11.5 49.0 reduce-scatter.1
  418.0 187.8 all-gather.1
where the time goes:
time: 701 us; the launch traced here: 700 us
  blocking collectives  343 us (49%)
  waiting for transfers between devices  257 us (37%)
  local copies, waits for them, and re-layouts  34.7 us (5%)
  other arithmetic  20.4 us (3%)
  starting transfers between devices  19.5 us (3%)
  between operations  14.3 us (2%)
  matrix products  11.6 us (2%)
    all_to_all x1, blocking collectives, local(): lax.all_to_all(outgoing, 'dp', split_axis=0, concat_axis=0, tiled=True)  297 us
    all_gather x1, waiting for transfers between devices, local(): lax.all_gather(activation, 'tensor', axis=2, tiled=True)  188 us
    all_to_all x1, waiting for transfers between devices, local(): lax.all_to_all(result, 'dp', split_axis=0, concat_axis=0, tiled=True)  43.3 us
    all_gather x1, blocking collectives, local(): full_rows = lax.all_gather(normed, 'tensor', axis=1, tiled=True)  29.5 us
    reduce_scatter x1, waiting for transfers between devices, local(): lax.psum_scatter(jnp.einsum('th,hd->dt', context, out_weight, preferred_e...  25.5 us
    all_to_all x1, starting transfers between devices, local(): lax.all_to_all(result, 'dp', split_axis=0, concat_axis=0, tiled=True)  19.4 us
    another operation x3, other arithmetic  18.2 us
    psum x1, blocking collectives, local(): squares = lax.psum(jnp.sum(attended * attended, axis=1), 'tensor')  16.2 us
  transfers between devices with their start and end apart: 3, of which 3 were waited for; matrix products, arithmetic and copies ran while one was open for 4% of the time, Pallas kernels for 0%

commit v1 on v0

--- a/solution.py
+++ b/solution.py
@@ -4,6 +4,12 @@
 from jax.sharding import PartitionSpec as P
 
 epsilon = 1e-06
+
+
+def packet_fit(xs, mesh_name):
+    tmp = lax.all_gather(xs, mesh_name)
+    x_now = jnp.sum(tmp, 0)
+    return x_now
 
 
 def local(
@@ -17,7 +23,7 @@
         tiled=True,
     )
     attended = residual_in + summed_proj.T
-    squares = lax.psum(jnp.sum(attended * attended, axis=1), "tensor")
+    squares = packet_fit(jnp.sum(attended * attended, axis=1), mesh_name="tensor")
     full_width = width_local * lax.axis_size("tensor")
     scaling = lax.rsqrt(squares / full_width + epsilon)
     normed = (attended * scaling[:, None] * norm_gain).astype(jnp.bfloat16)

time: 701 us -> 700 us (level)
    psum x1 -> x0, blocking collectives: 16.2 us -> none  [local(): squares = lax.psum(jnp.sum(attended * attended, axis=1), 'tensor')]
    all_gather x0 -> x1, blocking collectives: none -> 15.4 us  [packet_fit(): tmp = lax.all_gather(xs, mesh_name)]
where the time goes in v1:
time: 700 us; the launch traced here: 699 us
  blocking collectives  342 us (49%)
  waiting for transfers between devices  257 us (37%)
  local copies, waits for them, and re-layouts  34.7 us (5%)
  other arithmetic  20.4 us (3%)
  starting transfers between devices  19.5 us (3%)
  between operations  14.3 us (2%)
  matrix products  11.6 us (2%)
    all_to_all x1, blocking collectives, local(): lax.all_to_all(outgoing, 'dp', split_axis=0, concat_axis=0, tiled=True)  297 us
    all_gather x1, waiting for transfers between devices, local(): lax.all_gather(activation, 'tensor', axis=2, tiled=True)  188 us
    all_to_all x1, waiting for transfers between devices, local(): lax.all_to_all(result, 'dp', split_axis=0, concat_axis=0, tiled=True)  43.3 us
    all_gather x1, blocking collectives, local(): full_rows = lax.all_gather(normed, 'tensor', axis=1, tiled=True)  29.5 us
    reduce_scatter x1, waiting for transfers between devices, local(): lax.psum_scatter(jnp.einsum('th,hd->dt', context, out_weight, preferred_e...  25.5 us
    all_to_all x1, starting transfers between devices, local(): lax.all_to_all(result, 'dp', split_axis=0, concat_axis=0, tiled=True)  19.4 us
    another operation x3, other arithmetic  18.2 us
    all_gather x1, blocking collectives, packet_fit(): tmp = lax.all_gather(xs, mesh_name)  15.4 us
  transfers between devices with their start and end apart: 3, of which 3 were waited for; matrix products, arithmetic and copies ran while one was open for 4% of the time, Pallas kernels for 0%

profile of v1, /device:TPU:4, one launch (start us, length us, event | category | flops | bytes accessed | tf_op | source)
XLA Modules:
  0.0 699.1 jit_solution(8887564923995562923)
XLA Ops:
  7.2 0.0 copy-start
  7.2 0.0 copy-start.3
  7.2 0.0 reduce-scatter.2.cloned.1.call-start
  7.2 1.5 copy-done
  8.8 2.6 fusion.14
  11.4 0.0 copy-start.2
  11.4 0.0 copy-start.5
  11.4 0.0 reduce-scatter.2.cloned.1.call-update
  11.4 0.0 all-gather.4.cloned.1.call-start
  11.5 0.0 copy-done.3
  11.5 0.1 copy.27
  11.6 0.1 eq.29
  11.7 0.1 eq.25
  11.8 18.0 %reduce-window.6 = s32[64,8,128]{2,1,0:T(8,128)S(1)} reduce-window(s32[64,8,128]{2,1,0:T(8,128)S(1)} %fusion.8, s32[]{:T(128)} %constant.37.clone.1), window={size=1x1x128 pad=0_0x0_0x127_0}, to_apply=%region_4.5 | reduce-window | flops 8323072 | bytes 524292 | tf_op jit(solution)/shard_map/reduce-window
  29.8 0.1 slice.12
  29.9 0.1 copy.29
  30.1 0.1 copy.30
  30.2 0.1 copy.26
  30.3 0.1 mul.61
  30.4 0.0 copy-done.2
  30.4 0.1 copy.24
  30.5 0.1 broadcast_add_fusion
  30.7 0.1 fusion.7
  30.8 4.3 scatter_custom_fusion
  35.1 25.5 %reduce-scatter.2.cloned.1.call-done = f32[256,128]{1,0:T(8,128)} async-done(((f32[2048,128]{1,0:T(8,128)}), f32[256,128]{1,0:T(8,128)}) %reduce-scatter.2.cloned.1.call-update) | async-done | bytes 131088 | tf_op jit(solution)/shard_map/reduce_scatter | solution.py:19
  60.7 1.0 multiply_reduce_fusion
  61.6 15.4 %all-gather.1 = f32[8,1,128]{2,1,0:T(1,128)S(1)} all-gather(f32[1,1,128]{2,1,0:T(1,128)S(1)} %bitcast.53), channel_id=2, replica_groups=mesh['dp'=64,'tensor'=8] {'tensor'}, dimensions={0}, use_global_device_ids=true | all-gather | bytes 4608 | tf_op jit(solution)/shard_map/all_gather | solution.py:10
  77.0 0.0 copy-done.5
  77.0 0.1 multiply_convert_fusion.1
  77.1 29.5 %all_gather.14 = bf16[128,2048]{0,1:T(8,128)(2,1)S(1)} all-gather(bf16[128,256]{0,1:T(8,128)(2,1)S(1)} %multiply_convert_fusion.1), channel_id=1, replica_groups=mesh['dp'=64,'tensor'=8] {'tensor'}, dimensions={1}, use_global_device_ids=true | all-gather | bytes 589824 | tf_op jit(solution)/shard_map/all_gather | solution.py:47
  106.7 0.2 copy.35
  106.9 7.1 %gather_fusion = bf16[1536,2048]{1,0:T(8,128)(2,1)} fusion(bf16[129,2048]{1,0:T(8,128)(2,1)S(1)} %concatenate.3.clone, s32[2048]{0:T(1024)S(1)} %pad_clamp_fusion), kind=kCustom, calls=%fused_computation | custom fusion | bytes 12589056 | tf_op jit(solution)/shard_map/gather | solution.py:51
  114.0 0.0 copy-start.6
  114.0 296.8 %all_to_all.10 = bf16[64,24,2048]{2,1,0:T(8,128)(2,1)S(1)} all-to-all(bf16[64,24,2048]{2,1,0:T(8,128)(2,1)} %bitcast.47), channel_id=1, replica_groups=mesh['dp'=64,'tensor'=8] {'dp'}, dimensions={0} | all-to-all | bytes 12582912 | tf_op jit(solution)/shard_map/all_to_all | solution.py:52
  410.9 0.0 copy-done.6
  410.9 0.0 copy-start.7
  410.9 2.1 fusion.3
  412.9 0.0 copy-done.7
  412.9 2.3 multiply_convert_fusion
  415.2 1.8 copy.32
  417.0 0.0 all-gather.4.cloned.1.call-update
  417.0 0.0 copy-start.8
  417.1 188.0 %all-gather.4.cloned.1.call-done = bf16[64,24,1536]{0,1,2:T(8,128)(2,1)} async-done(((bf16[64,24,192]{0,1,2:T(8,128)(2,1)}), bf16[64,24,1536]{0,1,2:T(8,128)(2,1)}) %all-gather.4.cloned.1.call-update) | async-done | bytes 4718608 | tf_op jit(solution)/shard_map/all_gather | solution.py:58
  605.0 13.3 %copy.33 = bf16[64,24,1536]{2,1,0:T(8,128)(2,1)} copy(bf16[64,24,1536]{0,1,2:T(8,128)(2,1)} %all-gather.4.cloned.1.call-done) | data formatting | bytes 9437184 | tf_op jit(solution)/shard_map/all_gather | solution.py:58
  618.4 0.0 copy-done.8
  618.4 0.0 copy-start.4
  618.4 4.6 convolution_convert_fusion
  623.0 19.4 %all-to-all-start.1 = ((bf16[64,24,256]{2,1,0:T(8,128)(2,1)}), bf16[64,24,256]{2,1,0:T(8,128)(2,1)S(1)}, u32[]{:S(2)}, u32[]{:S(2)}) async-start(bf16[64,24,256]{2,1,0:T(8,128)(2,1)} %convolution_convert_fusion), calls=%async_computation.2 | async-start | bytes 1572864 | tf_op jit(solution)/shard_map/all_to_all | solution.py:63
  642.4 0.0 copy-done.4
  642.5 0.7 copy.25
  643.2 0.8 copy.34
  643.9 43.3 %all-to-all-done.1 = bf16[64,24,256]{2,1,0:T(8,128)(2,1)S(1)} async-done(((bf16[64,24,256]{2,1,0:T(8,128)(2,1)}), bf16[64,24,256]{2,1,0:T(8,128)(2,1)S(1)}, u32[]{:S(2)}, u32[]{:S(2)}) %all-to-all-start.1) | async-done | bytes 786464 | tf_op jit(solution)/shard_map/all_to_all | solution.py:63
  687.3 0.0 copy-start.1
  687.3 3.9 gather_fusion.1
  691.2 0.0 copy-done.1
  691.2 1.0 fusion
  (14 shorter events, 0.2 us)
Async XLA Ops:
  7.2 1.6 copy-start
  7.2 4.3 copy-start.3
  7.2 53.5 %reduce-scatter.2.cloned.1.call-start = ((), (), s32[]{:S(2)}) async-start(), calls=%async_computation.3 | async-start | bytes 1179648 | tf_op jit(solution)/shard_map/reduce_scatter | solution.py:19
  11.4 19.0 %copy-start.2 = (f32[128,256]{1,0:T(8,128)S(1)}, f32[128,256]{1,0:T(8,128)}, u32[]{:S(2)}) copy-start(f32[128,256]{1,0:T(8,128)} %param.11) | copy-start | bytes 393220
  11.4 65.6 %copy-start.5 = (f32[256]{0:T(256)S(1)}, f32[256]{0:T(256)}, u32[]{:S(2)}) copy-start(f32[256]{0:T(256)} %param.12) | copy-start | bytes 3076
  11.4 593.6 %all-gather.4.cloned.1.call-start = ((), (), s32[]{:S(2)}) async-start(), calls=%async_computation.4 | async-start | bytes 10616832 | tf_op jit(solution)/shard_map/all_gather | solution.py:58
  114.0 296.8 %copy-start.6 = (bf16[1,192,2048]{2,1,0:T(8,128)(2,1)S(1)}, bf16[1,192,2048]{2,1,0:T(8,128)(2,1)}, u32[]{:S(2)}) copy-start(bf16[1,192,2048]{2,1,0:T(8,128)(2,1)} %param.15) | copy-start | bytes 2359300
  410.9 2.1 copy-start.7
  417.0 201.3 %copy-start.8 = (bf16[1,1536,256]{2,1,0:T(8,128)(2,1)S(1)}, bf16[1,1536,256]{2,1,0:T(8,128)(2,1)}, u32[]{:S(2)}) copy-start(bf16[1,1536,256]{2,1,0:T(8,128)(2,1)} %param.17) | copy-start | bytes 2359300
  618.4 24.1 %copy-start.4 = (f32[128,8]{0,1:T(8,128)S(1)}, f32[128,8]{0,1:T(8,128)}, u32[]{:S(2)}) copy-start(f32[128,8]{0,1:T(8,128)} %param.14) | copy-start | bytes 12292
  623.0 64.3 %all-to-all-start.1 = ((bf16[64,24,256]{2,1,0:T(8,128)(2,1)}), bf16[64,24,256]{2,1,0:T(8,128)(2,1)S(1)}, u32[]{:S(2)}, u32[]{:S(2)}) async-start(bf16[64,24,256]{2,1,0:T(8,128)(2,1)} %convolution_convert_fusion), calls=%async_computation.2 | async-start | bytes 1572864 | tf_op jit(solution)/shard_map/all_to_all | solution.py:63
  687.3 3.9 copy-start.1
Sparse Core Ops, SparseCore 0:
  11.5 49.0 reduce-scatter.1
  417.2 187.8 all-gather.3
